TPU v7x, 256 devices: a whole 4x4x8 slice. The times are simulated.
256 devices in a mesh: ctx: 128 (over x_hi, y, z, core), head: 2 (over x_lo).
Axes of the slice: x: 4 (x_hi: 2, x_lo: 2; x = x_hi * 2 + x_lo), y: 4, z: 8, core: 2. Of those that a mesh axis runs over, the one named last changes fastest.
Arguments:
- queries: bfloat16 [32768, 2048], P(('ctx', 'head')), may hold values from -5 to 5
- keys: bfloat16 [32768, 2048], P(('ctx', 'head')), may hold values from -4 to 4
- values: bfloat16 [32768, 2048], P(('ctx', 'head')), may hold values from -6 to 6
- grad_out: bfloat16 [32768, 2048], P(('ctx', 'head')), may hold values from -6 to 6
- level_mask: int32 [256, 9], replicated, may hold values 0 or 1
Outputs:
- attended: bfloat16 [32768, 2048], P(('ctx', 'head'))
- grad_queries: bfloat16 [32768, 2048], P(('ctx', 'head'))
- grad_keys: bfloat16 [32768, 2048], P(('ctx', 'head'))
- grad_values: bfloat16 [32768, 2048], P(('ctx', 'head'))
All inputs are finite; a program needn't handle non-finite values.
Results may differ from a plain program's by a relative error of at most 0.011.
Values may be sent and summed in bfloat16 or wider, within the bound.
A program may use at most 128 MiB of HBM per device.

v0:
```python
import jax
import jax.numpy as jnp
from jax import lax
from jax.sharding import PartitionSpec as P

HD = 128
BLK = 128
LEVELS = 9


masked_value = -1e30


def passed_along(block, axis, distance):
    devices = range(lax.axis_size(axis))
    route = [(i - distance, i) for i in devices if i - distance in devices]
    return lax.ppermute(block, axis, route)


def head_major(flat, blk_count):
    return flat.reshape(blk_count, BLK, -1, HD).transpose(2, 0, 1, 3)


def token_major(stacked):
    head_count = stacked.shape[0]
    blk_count = stacked.shape[1]
    return stacked.transpose(1, 2, 0, 3).reshape(blk_count * BLK, head_count * HD)


def softmax_stats(scores):
    top_score = jnp.max(scores, -1, keepdims=True)
    return top_score[..., 0] + jnp.log(jnp.sum(jnp.exp(scores - top_score), -1))


def local(queries, keys, values, grad_out, level_mask):
    local_q, local_k, local_v, local_g = (
        lax.all_to_all(queries, "head", split_axis=1, concat_axis=0, tiled=True),
        lax.all_to_all(keys, "head", split_axis=1, concat_axis=0, tiled=True),
        lax.all_to_all(values, "head", split_axis=1, concat_axis=0, tiled=True),
        lax.all_to_all(grad_out, "head", split_axis=1, concat_axis=0, tiled=True),
    )
    tok_rows = local_q.shape[0]
    blk_count = tok_rows // BLK
    softmax_scale = HD ** (-0.5)
    ctx_index = lax.axis_index("ctx")
    ctx_size = lax.axis_size("ctx")
    q_heads = head_major(local_q, blk_count)
    k_heads = head_major(local_k, blk_count)
    v_heads = head_major(local_v, blk_count)
    g_heads = head_major(local_g, blk_count)
    head_count = q_heads.shape[0]
    prev_k, prev_v = passed_along((k_heads, v_heads), "ctx", 1)
    window_k = jnp.concatenate([prev_k, k_heads], 1)
    window_v = jnp.concatenate([prev_v, v_heads], 1)
    far_hops = []
    for level in range(LEVELS):
        distance = 2**level
        if distance > blk_count and distance // blk_count < ctx_size:
            far_hops.append((level, distance // blk_count))
    received = {}
    for level, hop_count in far_hops:
        received[level] = passed_along((k_heads, v_heads), "ctx", hop_count)
    empty_block = jnp.zeros_like(k_heads)
    key_parts = [k_heads]
    value_parts = [v_heads]
    for level in range(LEVELS):
        distance = 2**level
        if distance <= blk_count:
            key_parts.append(window_k[:, blk_count - distance : 2 * blk_count - distance])
            value_parts.append(window_v[:, blk_count - distance : 2 * blk_count - distance])
        elif level in received:
            key_parts.append(received[level][0])
            value_parts.append(received[level][1])
        else:
            key_parts.append(empty_block)
            value_parts.append(empty_block)
    set_shape = (head_count, blk_count, (1 + LEVELS) * BLK, HD)
    key_set = jnp.stack(key_parts, 2).reshape(set_shape)
    value_set = jnp.stack(value_parts, 2).reshape(set_shape)
    block_ids = ctx_index * blk_count + jnp.arange(blk_count, dtype=jnp.int32)
    level_dist = (2 ** jnp.arange(LEVELS)).astype(jnp.int32)
    mask_rows = lax.dynamic_slice_in_dim(level_mask, ctx_index * blk_count, blk_count, 0)
    permitted = (mask_rows == 1) & (block_ids[:, None] - level_dist[None, :] >= 0)
    causal = jnp.tril(jnp.ones((BLK, BLK), dtype=bool))
    level_part = jnp.broadcast_to(
        jnp.repeat(permitted, BLK, axis=1)[:, None, :], (blk_count, BLK, LEVELS * BLK)
    )
    own_part = jnp.broadcast_to(causal[None], (blk_count, BLK, BLK))
    score_mask = jnp.concatenate([own_part, level_part], -1)

    def query_head(operands):
        single_query_block, single_key_block, single_value_block, single_output_gradient = operands
        scores = (
            jnp.einsum(
                "lyp,lhp->lyh",
                single_query_block,
                single_key_block,
                preferred_element_type=jnp.float32,
            )
            * softmax_scale
        )
        scores = jnp.where(score_mask, scores, masked_value)
        lse = softmax_stats(scores)
        probs = jnp.exp(scores - lse[..., None])
        rounded_result = probs.astype(jnp.bfloat16)
        attended = jnp.einsum(
            "swc,scm->swm", rounded_result, single_value_block, preferred_element_type=jnp.float32
        ).astype(jnp.bfloat16)
        delta = jnp.sum(
            single_output_gradient.astype(jnp.float32) * attended.astype(jnp.float32), -1
        )
        probability_gradient = jnp.einsum(
            "lyp,lhp->lyh",
            single_output_gradient,
            single_value_block,
            preferred_element_type=jnp.float32,
        )
        score_gradient = (probs * (probability_gradient - delta[..., None])).astype(jnp.bfloat16)
        grad_q = (
            softmax_scale
            * jnp.einsum(
                "swc,scm->swm", score_gradient, single_key_block, preferred_element_type=jnp.float32
            )
        ).astype(jnp.bfloat16)
        key_term = softmax_scale * jnp.einsum(
            "yrt,yrl->ytl", score_gradient, single_query_block, preferred_element_type=jnp.float32
        )
        value_contribution = jnp.einsum(
            "yrt,yrl->ytl",
            rounded_result,
            single_output_gradient,
            preferred_element_type=jnp.float32,
        )
        return (attended, grad_q, lse, delta, key_term, value_contribution)

    attended, grad_q, lse_heads, delta_heads, key_term, value_contribution = lax.map(
        query_head, (q_heads, key_set, value_set, g_heads)
    )
    split_shape = (head_count, blk_count, 1 + LEVELS, BLK, HD)
    key_term = key_term.reshape(split_shape)
    value_contribution = value_contribution.reshape(split_shape)
    window_dk = jnp.zeros((head_count, 2 * blk_count, BLK, HD), jnp.float32)
    window_dv = jnp.zeros((head_count, 2 * blk_count, BLK, HD), jnp.float32)
    for level in range(LEVELS):
        distance = 2**level
        if distance <= blk_count:
            window_dk = window_dk.at[:, blk_count - distance : 2 * blk_count - distance].add(
                key_term[:, :, 1 + level]
            )
            window_dv = window_dv.at[:, blk_count - distance : 2 * blk_count - distance].add(
                value_contribution[:, :, 1 + level]
            )
    back_k, back_v = passed_along((window_dk[:, :blk_count], window_dv[:, :blk_count]), "ctx", -1)
    total_k = key_term[:, :, 0] + window_dk[:, blk_count:] + back_k
    total_v = value_contribution[:, :, 0] + window_dv[:, blk_count:] + back_v
    for level, hop_count in far_hops:
        got_k, got_v = passed_along(
            (key_term[:, :, 1 + level], value_contribution[:, :, 1 + level]), "ctx", -hop_count
        )
        total_k = total_k + got_k
        total_v = total_v + got_v
    return (
        lax.all_to_all(token_major(attended), "head", split_axis=0, concat_axis=1, tiled=True),
        lax.all_to_all(token_major(grad_q), "head", split_axis=0, concat_axis=1, tiled=True),
        lax.all_to_all(
            token_major(total_k.astype(jnp.bfloat16)),
            "head",
            split_axis=0,
            concat_axis=1,
            tiled=True,
        ),
        lax.all_to_all(
            token_major(total_v.astype(jnp.bfloat16)),
            "head",
            split_axis=0,
            concat_axis=1,
            tiled=True,
        ),
    )


def solution(mesh):
    placed = (
        P(("ctx", "head"), None),
        P(("ctx", "head"), None),
        P(("ctx", "head"), None),
        P(("ctx", "head"), None),
        P(),
    )
    return jax.shard_map(
        local,
        mesh=mesh,
        in_specs=placed,
        out_specs=(
            P(("ctx", "head"), None),
            P(("ctx", "head"), None),
            P(("ctx", "head"), None),
            P(("ctx", "head"), None),
        ),
        check_vma=False,
    )
```

profile of v0, /device:TPU:228, one launch (start us, length us, event | category | flops | bytes accessed | tf_op | source)
XLA Modules:
  0.0 650.3 jit_solution(3390915002633514403)
XLA Ops:
  2.8 3.5 all-to-all-start.2
  8.7 5.8 all-to-all-done.2
  14.5 3.5 all-to-all-start.1
  23.2 5.1 collective-permute-start.12
  33.7 3.5 all-to-all-start
  37.2 4.6 collective-permute-start
  48.1 21.0 %collective-permute-done = bf16[8,2,128,128]{2,3,0,1:T(8,128)(2,1)S(1)} collective-permute-done((bf16[8,2,128,128]{2,3,0,1:T(8,128)(2,1)S(1)}, bf16[8,2,128,128]{2,3,0,1:T(8,128)(2,1)S(1)}, u32[]{:S(2)}, u32[]{:S(2)}) %collective-permute-start) | collective-permute-done | bytes 524320 | tf_op jit(solution)/shard_map/ppermute | solution.py:17
  69.1 5.1 collective-permute-start.9
  78.2 19.8 %collective-permute-done.9 = bf16[8,2,128,128]{2,3,0,1:T(8,128)(2,1)S(1)} collective-permute-done((bf16[8,2,128,128]{2,3,0,1:T(8,128)(2,1)S(1)}, bf16[8,2,128,128]{2,3,0,1:T(8,128)(2,1)S(1)}, u32[]{:S(2)}, u32[]{:S(2)}) %collective-permute-start.9) | collective-permute-done | bytes 524320 | tf_op jit(solution)/shard_map/ppermute | solution.py:17
  97.9 4.3 collective-permute-start.5
  106.9 7.3 %collective-permute-start.1 = (bf16[8,2,128,128]{2,3,0,1:T(8,128)(2,1)S(1)}, bf16[8,2,128,128]{2,3,0,1:T(8,128)(2,1)S(1)}, u32[]{:S(2)}, u32[]{:S(2)}) collective-permute-start(bf16[8,2,128,128]{2,3,0,1:T(8,128)(2,1)S(1)} %bitcast.255), channel_id=1, source_target_pairs={{0,4},{2,6},{4,8},{6,10},{8,12},{10,14},{12,16},{14,18},{16,20},{1... | collective-permute-start | bytes 1572872 | tf_op jit(solution)/shard_map/ppermute | solution.py:17
  121.7 8.7 %collective-permute-done.1 = bf16[8,2,128,128]{2,3,0,1:T(8,128)(2,1)S(1)} collective-permute-done((bf16[8,2,128,128]{2,3,0,1:T(8,128)(2,1)S(1)}, bf16[8,2,128,128]{2,3,0,1:T(8,128)(2,1)S(1)}, u32[]{:S(2)}, u32[]{:S(2)}) %collective-permute-start.1) | collective-permute-done | bytes 524320 | tf_op jit(solution)/shard_map/ppermute | solution.py:17
  132.5 23.1 %collective-permute-done.2 = bf16[8,2,128,128]{2,3,0,1:T(8,128)(2,1)S(1)} collective-permute-done((bf16[8,2,128,128]{2,3,0,1:T(8,128)(2,1)S(1)}, bf16[8,2,128,128]{2,3,0,1:T(8,128)(2,1)S(1)}, u32[]{:S(2)}, u32[]{:S(2)}) %collective-permute-start.2) | collective-permute-done | bytes 524320 | tf_op jit(solution)/shard_map/ppermute | solution.py:17
  159.1 7.8 %copy.236 = bf16[8,2,10,128,128]{4,3,2,1,0:T(8,128)(2,1)} copy(bf16[8,2,10,128,128]{3,4,0,1,2:T(8,128)(2,1)} %broadcast_dynamic-update-slice_fusion) | data formatting | bytes 10485760 | tf_op jit(solution)/shard_map/stack | solution.py:79
  173.1 7.9 %copy.231 = bf16[8,2,10,128,128]{4,3,2,1,0:T(8,128)(2,1)} copy(bf16[8,2,10,128,128]{3,4,0,1,2:T(8,128)(2,1)} %broadcast_dynamic-update-slice_fusion.1) | data formatting | bytes 10485760 | tf_op jit(solution)/shard_map/stack | solution.py:78
  181.0 87.6 %while.20 = (s32[]{:T(128)}, bf16[8,2,128,128]{2,3,0,1:T(8,128)(2,1)}, bf16[8,2,128,128]{2,3,0,1:T(8,128)(2,1)}, f32[8,2,1280,128]{3,2,1,0:T(8,128)}, f32[8,2,12...) while((s32[]{:T(128)}, ...), condition=%wide.region_4.5_spmd, body=%wide.region_0.4_spmd.sunk | while | flops 508132864 | bytes 14958721 | solution.py:136
  268.6 4.6 fusion.62
  275.4 20.5 %collective-permute-start.27 = (f32[8,2,128,128]{3,0,2,1:T(8,128)}, f32[8,2,128,128]{3,0,2,1:T(8,128)}, u32[]{:S(2)}, u32[]{:S(2)}) collective-permute-start(f32[8,2,128,128]{3,0,2,1:T(8,128)} %bitcast.195), channel_id=1, source_target_pairs={{128,0},{130,2},{132,4},{134,6},{136,8},{138,10},{140,12},{142,14}... | collective-permute-start | bytes 3145736 | tf_op jit(solution)/shard_map/ppermute | solution.py:17
  301.3 4.0 collective-permute-start.22
  313.7 5.3 collective-permute-start.24
  325.4 77.6 %collective-permute-done.27 = f32[8,2,128,128]{3,0,2,1:T(8,128)} collective-permute-done((f32[8,2,128,128]{3,0,2,1:T(8,128)}, f32[8,2,128,128]{3,0,2,1:T(8,128)}, u32[]{:S(2)}, u32[]{:S(2)}) %collective-permute-start.27) | collective-permute-done | bytes 1048608 | tf_op jit(solution)/shard_map/ppermute | solution.py:17
  406.9 5.8 collective-permute-start.20
  427.6 7.0 %collective-permute-done.25 = f32[8,2,128,128]{3,0,2,1:T(8,128)} collective-permute-done((f32[8,2,128,128]{3,0,2,1:T(8,128)}, f32[8,2,128,128]{3,0,2,1:T(8,128)}, u32[]{:S(2)}, u32[]{:S(2)}) %collective-permute-start.25) | collective-permute-done | bytes 1048608 | tf_op jit(solution)/shard_map/ppermute | solution.py:17
  434.6 4.2 collective-permute-start.16
  438.8 69.8 %collective-permute-done.26 = f32[8,2,128,128]{3,0,2,1:T(8,128)} collective-permute-done((f32[8,2,128,128]{3,0,2,1:T(8,128)}, f32[8,2,128,128]{3,0,2,1:T(8,128)}, u32[]{:S(2)}, u32[]{:S(2)}) %collective-permute-start.26) | collective-permute-done | bytes 1048608 | tf_op jit(solution)/shard_map/ppermute | solution.py:17
  510.5 51.9 %collective-permute-done.20 = f32[8,2,128,128]{3,0,2,1:T(8,128)} collective-permute-done((f32[8,2,128,128]{3,0,2,1:T(8,128)S(1)}, f32[8,2,128,128]{3,0,2,1:T(8,128)}, u32[]{:S(2)}, u32[]{:S(2)}) %collective-permute-start.20) | collective-permute-done | bytes 1048608 | tf_op jit(solution)/shard_map/ppermute | solution.py:17
  566.3 49.7 %all_to_all.140 = bf16[2,128,1024]{1,2,0:T(8,128)(2,1)} all-to-all(bf16[2,128,1024]{1,2,0:T(8,128)(2,1)} %bitcast.49), channel_id=1, replica_groups=mesh['ctx'=128,'head'=2] {'head'}, dimensions={0} | all-to-all | bytes 1048576 | tf_op jit(solution)/shard_map/all_to_all | solution.py:163
  616.1 4.2 all-to-all-start.5
  620.3 4.8 fusion.57
  628.4 3.5 all-to-all-start.7
  632.0 4.4 fusion.58
  639.0 3.5 all-to-all-start.6
  (214 shorter events, 196.8 us)
Async XLA Ops:
  14.5 19.2 %all-to-all-start.1 = ((bf16[128,2,1024]{0,2,1:T(8,128)(2,1)}), bf16[128,2,1024]{0,2,1:T(8,128)(2,1)S(1)}, u32[]{:S(2)}, u32[]{:S(2)}) async-start(bf16[128,2,1024]{0,2,1:T(8,128)(2,1)} %bitcast.12), calls=%async_computation.1 | async-start | bytes 1048576 | tf_op jit(solution)/shard_map/all_to_all | solution.py:38
  18.0 25.5 %collective-permute-start.7 = (bf16[8,2,128,128]{2,3,0,1:T(8,128)(2,1)S(1)}, bf16[8,2,128,128]{2,3,0,1:T(8,128)(2,1)S(1)}, u32[]{:S(2)}, u32[]{:S(2)}) collective-permute-start(bf16[8,2,128,128]{2,3,0,1:T(8,128)(2,1)S(1)} %bitcast.259), channel_id=1, source_target_pairs={{0,2},{2,4},{4,6},{6,8},{8,10},{10,12},{12,14},{14,16},{16,18},{18... | collective-permute-start | bytes 1572872 | tf_op jit(solution)/shard_map/ppermute | solution.py:17
  23.2 93.0 %collective-permute-start.12 = (bf16[8,2,128,128]{2,3,0,1:T(8,128)(2,1)S(1)}, bf16[8,2,128,128]{2,3,0,1:T(8,128)(2,1)S(1)}, u32[]{:S(2)}, u32[]{:S(2)}) collective-permute-start(bf16[8,2,128,128]{2,3,0,1:T(8,128)(2,1)S(1)} %bitcast.260), channel_id=1, source_target_pairs={{0,64},{2,66},{4,68},{6,70},{8,72},{10,74},{12,76},{14,78},{16,80}... | collective-permute-start | bytes 1572872 | tf_op jit(solution)/shard_map/ppermute | solution.py:17
  28.3 78.6 %collective-permute-start.11 = (bf16[8,2,128,128]{2,3,0,1:T(8,128)(2,1)S(1)}, bf16[8,2,128,128]{2,3,0,1:T(8,128)(2,1)}, u32[]{:S(2)}, u32[]{:S(2)}) collective-permute-start(bf16[8,2,128,128]{2,3,0,1:T(8,128)(2,1)S(1)} %bitcast.261), channel_id=1, source_target_pairs={{0,32},{2,34},{4,36},{6,38},{8,40},{10,42},{12,44},{14,46},{16,48}... | collective-permute-start | bytes 1572872 | tf_op jit(solution)/shard_map/ppermute | solution.py:17
  30.9 72.2 %collective-permute-start.10 = (bf16[8,2,128,128]{2,3,0,1:T(8,128)(2,1)S(1)}, bf16[8,2,128,128]{2,3,0,1:T(8,128)(2,1)}, u32[]{:S(2)}, u32[]{:S(2)}) collective-permute-start(bf16[8,2,128,128]{2,3,0,1:T(8,128)(2,1)S(1)} %bitcast.262), channel_id=1, source_target_pairs={{0,16},{2,18},{4,20},{6,22},{8,24},{10,26},{12,28},{14,30},{16,32}... | collective-permute-start | bytes 1572872 | tf_op jit(solution)/shard_map/ppermute | solution.py:17
  33.7 134.1 %all-to-all-start = ((bf16[128,2,1024]{0,2,1:T(8,128)(2,1)}), bf16[128,2,1024]{0,2,1:T(8,128)(2,1)S(1)}, u32[]{:S(2)}, u32[]{:S(2)}) async-start(bf16[128,2,1024]{0,2,1:T(8,128)(2,1)} %bitcast.8), calls=%async_computation | async-start | bytes 1048576 | tf_op jit(solution)/shard_map/all_to_all | solution.py:37
  37.2 31.9 %collective-permute-start = (bf16[8,2,128,128]{2,3,0,1:T(8,128)(2,1)S(1)}, bf16[8,2,128,128]{2,3,0,1:T(8,128)(2,1)S(1)}, u32[]{:S(2)}, u32[]{:S(2)}) collective-permute-start(bf16[8,2,128,128]{2,3,0,1:T(8,128)(2,1)S(1)} %bitcast.250), channel_id=1, source_target_pairs={{0,2},{2,4},{4,6},{6,8},{8,10},{10,12},{12,14},{14,16},{16,18},{18... | collective-permute-start | bytes 1572872 | tf_op jit(solution)/shard_map/ppermute | solution.py:17
  43.5 32.5 %collective-permute-start.8 = (bf16[8,2,128,128]{2,3,0,1:T(8,128)(2,1)S(1)}, bf16[8,2,128,128]{2,3,0,1:T(8,128)(2,1)S(1)}, u32[]{:S(2)}, u32[]{:S(2)}) collective-permute-start(bf16[8,2,128,128]{2,3,0,1:T(8,128)(2,1)S(1)} %bitcast.264), channel_id=1, source_target_pairs={{0,4},{2,6},{4,8},{6,10},{8,12},{10,14},{12,16},{14,18},{16,20},{1... | collective-permute-start | bytes 1572872 | tf_op jit(solution)/shard_map/ppermute | solution.py:17
  69.1 28.8 %collective-permute-start.9 = (bf16[8,2,128,128]{2,3,0,1:T(8,128)(2,1)S(1)}, bf16[8,2,128,128]{2,3,0,1:T(8,128)(2,1)S(1)}, u32[]{:S(2)}, u32[]{:S(2)}) collective-permute-start(bf16[8,2,128,128]{2,3,0,1:T(8,128)(2,1)S(1)} %bitcast.266), channel_id=1, source_target_pairs={{0,8},{2,10},{4,12},{6,14},{8,16},{10,18},{12,20},{14,22},{16,24},... | collective-permute-start | bytes 1572872 | tf_op jit(solution)/shard_map/ppermute | solution.py:17
  76.0 42.9 %collective-permute-start.13 = (bf16[8,2,128,128]{2,3,0,1:T(8,128)(2,1)S(1)}, bf16[8,2,128,128]{2,3,0,1:T(8,128)(2,1)S(1)}, u32[]{:S(2)}, u32[]{:S(2)}) collective-permute-start(bf16[8,2,128,128]{2,3,0,1:T(8,128)(2,1)S(1)} %bitcast.267), channel_id=1, source_target_pairs={{0,128},{2,130},{4,132},{6,134},{8,136},{10,138},{12,140},{14,142}... | collective-permute-start | bytes 1572872 | tf_op jit(solution)/shard_map/ppermute | solution.py:17
  97.9 69.0 %collective-permute-start.5 = (bf16[8,2,128,128]{2,3,0,1:T(8,128)(2,1)S(1)}, bf16[8,2,128,128]{2,3,0,1:T(8,128)(2,1)S(1)}, u32[]{:S(2)}, u32[]{:S(2)}) collective-permute-start(bf16[8,2,128,128]{2,3,0,1:T(8,128)(2,1)S(1)} %bitcast.253), channel_id=1, source_target_pairs={{0,64},{2,66},{4,68},{6,70},{8,72},{10,74},{12,76},{14,78},{16,80}... | collective-permute-start | bytes 1572872 | tf_op jit(solution)/shard_map/ppermute | solution.py:17
  103.1 54.3 %collective-permute-start.4 = (bf16[8,2,128,128]{2,3,0,1:T(8,128)(2,1)S(1)}, bf16[8,2,128,128]{2,3,0,1:T(8,128)(2,1)S(1)}, u32[]{:S(2)}, u32[]{:S(2)}) collective-permute-start(bf16[8,2,128,128]{2,3,0,1:T(8,128)(2,1)S(1)} %bitcast.254), channel_id=1, source_target_pairs={{0,32},{2,34},{4,36},{6,38},{8,40},{10,42},{12,44},{14,46},{16,48}... | collective-permute-start | bytes 1572872 | tf_op jit(solution)/shard_map/ppermute | solution.py:17
  106.9 23.5 %collective-permute-start.1 = (bf16[8,2,128,128]{2,3,0,1:T(8,128)(2,1)S(1)}, bf16[8,2,128,128]{2,3,0,1:T(8,128)(2,1)S(1)}, u32[]{:S(2)}, u32[]{:S(2)}) collective-permute-start(bf16[8,2,128,128]{2,3,0,1:T(8,128)(2,1)S(1)} %bitcast.255), channel_id=1, source_target_pairs={{0,4},{2,6},{4,8},{6,10},{8,12},{10,14},{12,16},{14,18},{16,20},{1... | collective-permute-start | bytes 1572872 | tf_op jit(solution)/shard_map/ppermute | solution.py:17
  116.2 39.5 %collective-permute-start.2 = (bf16[8,2,128,128]{2,3,0,1:T(8,128)(2,1)S(1)}, bf16[8,2,128,128]{2,3,0,1:T(8,128)(2,1)S(1)}, u32[]{:S(2)}, u32[]{:S(2)}) collective-permute-start(bf16[8,2,128,128]{2,3,0,1:T(8,128)(2,1)S(1)} %bitcast.256), channel_id=1, source_target_pairs={{0,8},{2,10},{4,12},{6,14},{8,16},{10,18},{12,20},{14,22},{16,24},... | collective-permute-start | bytes 1572872 | tf_op jit(solution)/shard_map/ppermute | solution.py:17
  119.0 37.6 %collective-permute-start.3 = (bf16[8,2,128,128]{2,3,0,1:T(8,128)(2,1)S(1)}, bf16[8,2,128,128]{2,3,0,1:T(8,128)(2,1)S(1)}, u32[]{:S(2)}, u32[]{:S(2)}) collective-permute-start(bf16[8,2,128,128]{2,3,0,1:T(8,128)(2,1)S(1)} %bitcast.257), channel_id=1, source_target_pairs={{0,16},{2,18},{4,20},{6,22},{8,24},{10,26},{12,28},{14,30},{16,32}... | collective-permute-start | bytes 1572872 | tf_op jit(solution)/shard_map/ppermute | solution.py:17
  130.4 40.9 %collective-permute-start.6 = (bf16[8,2,128,128]{2,3,0,1:T(8,128)(2,1)S(1)}, bf16[8,2,128,128]{2,3,0,1:T(8,128)(2,1)S(1)}, u32[]{:S(2)}, u32[]{:S(2)}) collective-permute-start(bf16[8,2,128,128]{2,3,0,1:T(8,128)(2,1)S(1)} %bitcast.258), channel_id=1, source_target_pairs={{0,128},{2,130},{4,132},{6,134},{8,136},{10,138},{12,140},{14,142}... | collective-permute-start | bytes 1572872 | tf_op jit(solution)/shard_map/ppermute | solution.py:17
  167.8 13.2 %all-to-all-start.3 = ((bf16[128,2,1024]{0,2,1:T(8,128)(2,1)}), bf16[128,2,1024]{0,2,1:T(8,128)(2,1)S(1)}, u32[]{:S(2)}, u32[]{:S(2)}) async-start(bf16[128,2,1024]{0,2,1:T(8,128)(2,1)} %bitcast.44), calls=%async_computation.3 | async-start | bytes 1048576 | tf_op jit(solution)/shard_map/all_to_all | solution.py:40
  275.4 127.6 %collective-permute-start.27 = (f32[8,2,128,128]{3,0,2,1:T(8,128)}, f32[8,2,128,128]{3,0,2,1:T(8,128)}, u32[]{:S(2)}, u32[]{:S(2)}) collective-permute-start(f32[8,2,128,128]{3,0,2,1:T(8,128)} %bitcast.195), channel_id=1, source_target_pairs={{128,0},{130,2},{132,4},{134,6},{136,8},{138,10},{140,12},{142,14}... | collective-permute-start | bytes 3145736 | tf_op jit(solution)/shard_map/ppermute | solution.py:17
  297.5 107.4 %collective-permute-start.21 = (f32[8,2,128,128]{3,0,2,1:T(8,128)}, f32[8,2,128,128]{3,0,2,1:T(8,128)}, u32[]{:S(2)}, u32[]{:S(2)}) collective-permute-start(f32[8,2,128,128]{3,0,2,1:T(8,128)} %fusion.52), channel_id=1, source_target_pairs={{2,0},{4,2},{6,4},{8,6},{10,8},{12,10},{14,12},{16,14},{18,16},{20... | collective-permute-start | bytes 3145736 | tf_op jit(solution)/shard_map/ppermute | solution.py:17
  301.3 105.6 %collective-permute-start.22 = (f32[8,2,128,128]{3,0,2,1:T(8,128)}, f32[8,2,128,128]{3,0,2,1:T(8,128)}, u32[]{:S(2)}, u32[]{:S(2)}) collective-permute-start(f32[8,2,128,128]{3,0,2,1:T(8,128)} %bitcast.200), channel_id=1, source_target_pairs={{4,0},{6,2},{8,4},{10,6},{12,8},{14,10},{16,12},{18,14},{20,16},{2... | collective-permute-start | bytes 3145736 | tf_op jit(solution)/shard_map/ppermute | solution.py:17
  306.8 109.0 %collective-permute-start.23 = (f32[8,2,128,128]{3,0,2,1:T(8,128)}, f32[8,2,128,128]{3,0,2,1:T(8,128)}, u32[]{:S(2)}, u32[]{:S(2)}) collective-permute-start(f32[8,2,128,128]{3,0,2,1:T(8,128)} %bitcast.199), channel_id=1, source_target_pairs={{8,0},{10,2},{12,4},{14,6},{16,8},{18,10},{20,12},{22,14},{24,16},... | collective-permute-start | bytes 3145736 | tf_op jit(solution)/shard_map/ppermute | solution.py:17
  313.7 112.0 %collective-permute-start.24 = (f32[8,2,128,128]{3,0,2,1:T(8,128)}, f32[8,2,128,128]{3,0,2,1:T(8,128)}, u32[]{:S(2)}, u32[]{:S(2)}) collective-permute-start(f32[8,2,128,128]{3,0,2,1:T(8,128)} %bitcast.198), channel_id=1, source_target_pairs={{16,0},{18,2},{20,4},{22,6},{24,8},{26,10},{28,12},{30,14},{32,16}... | collective-permute-start | bytes 3145736 | tf_op jit(solution)/shard_map/ppermute | solution.py:17
  403.1 31.6 %collective-permute-start.25 = (f32[8,2,128,128]{3,0,2,1:T(8,128)}, f32[8,2,128,128]{3,0,2,1:T(8,128)}, u32[]{:S(2)}, u32[]{:S(2)}) collective-permute-start(f32[8,2,128,128]{3,0,2,1:T(8,128)} %bitcast.274), channel_id=1, source_target_pairs={{32,0},{34,2},{36,4},{38,6},{40,8},{42,10},{44,12},{46,14},{48,16}... | collective-permute-start | bytes 3145736 | tf_op jit(solution)/shard_map/ppermute | solution.py:17
  405.0 103.6 %collective-permute-start.26 = (f32[8,2,128,128]{3,0,2,1:T(8,128)}, f32[8,2,128,128]{3,0,2,1:T(8,128)}, u32[]{:S(2)}, u32[]{:S(2)}) collective-permute-start(f32[8,2,128,128]{3,0,2,1:T(8,128)} %bitcast.273), channel_id=1, source_target_pairs={{64,0},{66,2},{68,4},{70,6},{72,8},{74,10},{76,12},{78,14},{80,16}... | collective-permute-start | bytes 3145736 | tf_op jit(solution)/shard_map/ppermute | solution.py:17
  406.9 155.5 %collective-permute-start.20 = (f32[8,2,128,128]{3,0,2,1:T(8,128)S(1)}, f32[8,2,128,128]{3,0,2,1:T(8,128)}, u32[]{:S(2)}, u32[]{:S(2)}) collective-permute-start(f32[8,2,128,128]{3,0,2,1:T(8,128)S(1)} %bitcast.275), channel_id=1, source_target_pairs={{128,0},{130,2},{132,4},{134,6},{136,8},{138,10},{140,12},{142,14}... | collective-permute-start | bytes 3145736 | tf_op jit(solution)/shard_map/ppermute | solution.py:17
  415.8 148.5 %collective-permute-start.14 = (f32[8,2,128,128]{3,0,2,1:T(8,128)S(1)}, f32[8,2,128,128]{3,0,2,1:T(8,128)}, u32[]{:S(2)}, u32[]{:S(2)}) collective-permute-start(f32[8,2,128,128]{3,0,2,1:T(8,128)S(1)} %fusion.42), channel_id=1, source_target_pairs={{2,0},{4,2},{6,4},{8,6},{10,8},{12,10},{14,12},{16,14},{18,16},{20... | collective-permute-start | bytes 3145736 | tf_op jit(solution)/shard_map/ppermute | solution.py:17
  425.7 206.2 %collective-permute-start.15 = (f32[8,2,128,128]{3,0,2,1:T(8,128)}, f32[8,2,128,128]{3,0,2,1:T(8,128)}, u32[]{:S(2)}, u32[]{:S(2)}) collective-permute-start(f32[8,2,128,128]{3,0,2,1:T(8,128)} %bitcast.207), channel_id=1, source_target_pairs={{4,0},{6,2},{8,4},{10,6},{12,8},{14,10},{16,12},{18,14},{20,16},{2... | collective-permute-start | bytes 3145736 | tf_op jit(solution)/shard_map/ppermute | solution.py:17
  434.6 197.2 %collective-permute-start.16 = (f32[8,2,128,128]{3,0,2,1:T(8,128)}, f32[8,2,128,128]{3,0,2,1:T(8,128)}, u32[]{:S(2)}, u32[]{:S(2)}) collective-permute-start(f32[8,2,128,128]{3,0,2,1:T(8,128)} %bitcast.206), channel_id=1, source_target_pairs={{8,0},{10,2},{12,4},{14,6},{16,8},{18,10},{20,12},{22,14},{24,16},... | collective-permute-start | bytes 3145736 | tf_op jit(solution)/shard_map/ppermute | solution.py:17
  508.6 123.3 %collective-permute-start.17 = (f32[8,2,128,128]{3,0,2,1:T(8,128)}, f32[8,2,128,128]{3,0,2,1:T(8,128)}, u32[]{:S(2)}, u32[]{:S(2)}) collective-permute-start(f32[8,2,128,128]{3,0,2,1:T(8,128)} %bitcast.205), channel_id=1, source_target_pairs={{16,0},{18,2},{20,4},{22,6},{24,8},{26,10},{28,12},{30,14},{32,16}... | collective-permute-start | bytes 3145736 | tf_op jit(solution)/shard_map/ppermute | solution.py:17
  562.5 69.5 %collective-permute-start.18 = (f32[8,2,128,128]{3,0,2,1:T(8,128)}, f32[8,2,128,128]{3,0,2,1:T(8,128)}, u32[]{:S(2)}, u32[]{:S(2)}) collective-permute-start(f32[8,2,128,128]{3,0,2,1:T(8,128)} %bitcast.204), channel_id=1, source_target_pairs={{32,0},{34,2},{36,4},{38,6},{40,8},{42,10},{44,12},{46,14},{48,16}... | collective-permute-start | bytes 3145736 | tf_op jit(solution)/shard_map/ppermute | solution.py:17
  564.4 67.5 %collective-permute-start.19 = (f32[8,2,128,128]{3,0,2,1:T(8,128)}, f32[8,2,128,128]{3,0,2,1:T(8,128)}, u32[]{:S(2)}, u32[]{:S(2)}) collective-permute-start(f32[8,2,128,128]{3,0,2,1:T(8,128)} %bitcast.203), channel_id=1, source_target_pairs={{64,0},{66,2},{68,4},{70,6},{72,8},{74,10},{76,12},{78,14},{80,16}... | collective-permute-start | bytes 3145736 | tf_op jit(solution)/shard_map/ppermute | solution.py:17
  616.1 12.3 %all-to-all-start.5 = ((bf16[2,128,1024]{1,2,0:T(8,128)(2,1)}), bf16[2,128,1024]{1,2,0:T(8,128)(2,1)}, u32[]{:S(2)}, u32[]{:S(2)}) async-start(bf16[2,128,1024]{1,2,0:T(8,128)(2,1)} %bitcast.276), calls=%async_computation.5 | async-start | bytes 1048576 | tf_op jit(solution)/shard_map/all_to_all | solution.py:164
  (11 other events, 308.4 us)
where the time goes:
time: 654 us; the launch traced here: 650 us
  waiting for transfers between devices  292 us (45%)
  starting transfers between devices  128 us (20%)
  local copies, waits for them, and re-layouts  84.7 us (13%)
  matrix products  78.2 us (12%)
  blocking collectives  49.7 us (8%)
  other arithmetic  16.4 us (3%)
    ppermute x28, waiting for transfers between devices, passed_along(): return lax.ppermute(block, axis, route)  281 us
    ppermute x28, starting transfers between devices, passed_along(): return lax.ppermute(block, axis, route)  102 us
    unnamed x57, local copies, waits for them, and re-layouts  50 us
    all_to_all x1, blocking collectives, local(): lax.all_to_all(token_major(attended), 'head', split_axis=0, concat_axis=1...  49.7 us
    dot_general x8, matrix products, query_head(): jnp.einsum('swc,scm->swm', rounded_result, single_value_block, preferred_...  17.6 us
  transfers between devices with their start and end apart: 35, of which 13 were waited for; matrix products, arithmetic and copies ran while one was open for 12% of the time, Pallas kernels for 0%

commit v1 on v0

v1 whole, which is shorter than its diff:
```python
import jax
import jax.numpy as jnp
from jax import lax
from jax.experimental import pallas as pl
from jax.experimental.pallas import tpu as pltpu
from jax.sharding import PartitionSpec as P

HD = 128
BLK = 128
LEVELS = 9
NB = 256
H = 16
FAR = 8
OWN = FAR
SLOTS = FAR + 1
WIDE = SLOTS * BLK
NEG = -1e30
SCALE = HD ** (-0.5)
LOG2E = 1.4426950408889634
MESH = pl.DeviceIdType.MESH

RELAY1 = 2
RELAY2 = 4
QUERY = 6
KEY = 7


def dot_nt(a, b):
    return lax.dot_general(a, b, (((1,), (1,)), ((), ())), preferred_element_type=jnp.float32)


def dot_nn(a, b):
    return lax.dot_general(a, b, (((1,), (0,)), ((), ())), preferred_element_type=jnp.float32)


def place(block):
    return (block // 2, block % 2)


def kernel(
    q_hbm, k_hbm, v_hbm, g_hbm, lm_ref,
    o_hbm, dq_hbm, dk_hbm, dv_hbm,
    kv, qg, st, p_s, pb, dsb, ob, bias,
    load_sem, send_sem, recv_sem, st_send, st_recv, out_sem,
):
    me = lax.axis_index("ctx") * 2 + lax.axis_index("head")
    bufs = (kv, qg)
    index = (me, NB - 1 - me)

    def real(side, m):
        return m if side == 0 else NB - 1 - m

    def copy(side, src, level, head, target):
        buf = bufs[side]
        return pltpu.make_async_remote_copy(
            src_ref=buf.at[head, :, src],
            dst_ref=buf.at[head, :, level],
            send_sem=send_sem.at[side, level],
            recv_sem=recv_sem.at[side, level, head],
            device_id=place(real(side, target)),
            device_id_type=MESH,
        )

    def send(side, src, level, head, target, cond):
        @pl.when(cond)
        def _():
            copy(side, src, level, head, target).start()

    def wait_recv(side, level, head):
        @pl.when(index[side] >= 2**level)
        def _():
            copy(side, OWN, level, head, index[side]).wait_recv()

    def loads(head):
        cols = pl.ds(pl.multiple_of(head * HD, HD), HD)
        return [
            pltpu.make_async_copy(k_hbm.at[:, cols], kv.at[head, 0, OWN], load_sem.at[0, head]),
            pltpu.make_async_copy(v_hbm.at[:, cols], kv.at[head, 1, OWN], load_sem.at[1, head]),
            pltpu.make_async_copy(q_hbm.at[:, cols], qg.at[head, 0, OWN], load_sem.at[2, head]),
            pltpu.make_async_copy(g_hbm.at[:, cols], qg.at[head, 1, OWN], load_sem.at[3, head]),
        ]

    @pl.loop(0, H)
    def _(head):
        for c in loads(head):
            c.start()

    for side in range(2):
        for level in range(FAR):

            @pl.when(index[side] < 2**level)
            def _(side=side, level=level):
                @pl.loop(0, H)
                def _(head):
                    bufs[side][head, :, level] = jnp.zeros((2, BLK, HD), jnp.bfloat16)
                    if side == 1:
                        st[head, level] = jnp.zeros((8, BLK), jnp.float32)

    for level in range(FAR):
        d = 2**level
        bias[0, level] = jnp.where((lm_ref[me, level] == 1) & (me >= d), 0.0, NEG)
        later = jnp.minimum(me + d, NB - 1)
        bias[1, level] = jnp.where((lm_ref[later, level] == 1) & (me + d < NB), 0.0, NEG)

    barrier = pltpu.get_barrier_semaphore()
    count = jnp.where((me % 4 == 0) | (me % 4 == 3), 1, 0)
    for level in range(FAR):
        d = 2**level
        count = count + jnp.where(me >= d, 1, 0) + jnp.where(me + d < NB, 1, 0)

        @pl.when(me >= d)
        def _(d=d):
            pl.semaphore_signal(barrier, inc=1, device_id=place(me - d), device_id_type=MESH)

        @pl.when(me + d < NB)
        def _(d=d):
            pl.semaphore_signal(barrier, inc=1, device_id=place(me + d), device_id_type=MESH)

    @pl.when(me % 4 == 0)
    def _():
        pl.semaphore_signal(barrier, inc=1, device_id=place(me + 3), device_id_type=MESH)

    @pl.when(me % 4 == 3)
    def _():
        pl.semaphore_signal(barrier, inc=1, device_id=place(me - 3), device_id_type=MESH)

    pl.semaphore_wait(barrier, count)

    def sends_own(side):
        m = index[side]
        return [
            (2, m + 4, m + 4 < NB),
            (5, m + 32, m + 32 < NB),
            (7, m + 128, m + 128 < NB),
            (0, m + 1, m % 4 != 3),
            (1, m + 2, m % 4 < 2),
        ]

    def sends_near(side):
        m = index[side]
        return [
            (3, m + 4, (m >= 4) & (m + 4 < NB)),
            (0, m - 3, (m >= 4) & (m % 4 == 3)),
            (1, m - 2, (m >= 4) & (m % 4 >= 2)),
        ]

    def sends_mid(side):
        m = index[side]
        return [(6, m + 32, (m >= 32) & (m + 32 < NB))]

    def sends_far(side):
        m = index[side]
        return [(4, m + 8, (m >= 8) & (m + 8 < NB))]

    def own(head):
        for c in loads(head):
            c.wait()
        for i in range(5):
            for side in range(2):
                level, target, cond = sends_own(side)[i]
                send(side, OWN, level, head, target, cond)

    def relay1(head):
        for side in range(2):
            wait_recv(side, 2, head)
            for level, target, cond in sends_near(side):
                send(side, 2, level, head, target, cond)
        for side in range(2):
            wait_recv(side, 5, head)
            for level, target, cond in sends_mid(side):
                send(side, 5, level, head, target, cond)

    def relay2(head):
        for side in range(2):
            wait_recv(side, 3, head)
            for level, target, cond in sends_far(side):
                send(side, 3, level, head, target, cond)

    def stat_copy(level, head):
        return pltpu.make_async_remote_copy(
            src_ref=st.at[head, OWN],
            dst_ref=st.at[head, level],
            send_sem=st_send.at[level],
            recv_sem=st_recv.at[level, head],
            device_id=place(me - 2**level),
            device_id_type=MESH,
        )

    def stores(head, which):
        cols = pl.ds(pl.multiple_of(head * HD, HD), HD)
        return [
            pltpu.make_async_copy(ob.at[i, head], (o_hbm, dq_hbm, dk_hbm, dv_hbm)[i].at[:, cols], out_sem.at[i, head])
            for i in which
        ]

    row_id = lax.broadcasted_iota(jnp.int32, (BLK, BLK), 0)
    col_id = lax.broadcasted_iota(jnp.int32, (BLK, BLK), 1)

    def span(slot):
        return pl.ds(slot * BLK, BLK)

    def query_side(head):
        for level in (0, 1, 7, 6, 4):
            wait_recv(0, level, head)
        q = qg[head, 0, OWN]
        g = qg[head, 1, OWN]
        top = None
        for slot in range(SLOTS):
            s = dot_nt(q, kv[head, 0, slot]) * (SCALE * LOG2E)
            s = jnp.where(row_id >= col_id, s, NEG) if slot == OWN else s + bias[0, slot]
            p_s[:, span(slot)] = s
            top = s if top is None else jnp.maximum(top, s)
        top = jnp.max(top, axis=1, keepdims=True)
        total = None
        for slot in range(SLOTS):
            p = jnp.exp2(p_s[:, span(slot)] - top)
            p_s[:, span(slot)] = p
            pb[:, span(slot)] = p.astype(jnp.bfloat16)
            total = p if total is None else total + p
        total = jnp.sum(total, axis=1, keepdims=True)
        inverse = 1.0 / total
        o = dot_nn(pb[...], kv[head, 1].reshape(WIDE, HD)) * inverse
        o = o.astype(jnp.bfloat16)
        ob[0, head] = o
        delta = jnp.sum(g.astype(jnp.float32) * o.astype(jnp.float32), axis=1, keepdims=True)
        lse = top + jnp.log2(total)
        st[head, OWN] = jnp.where(col_id == 0, lse, delta).T[:8]
        for level in range(FAR):

            @pl.when(me >= 2**level)
            def _(level=level):
                stat_copy(level, head).start()

        for slot in range(SLOTS):
            dp = dot_nt(g, kv[head, 1, slot])
            dsb[:, span(slot)] = (p_s[:, span(slot)] * (dp - delta)).astype(jnp.bfloat16)
        dq = dot_nn(dsb[...], kv[head, 0].reshape(WIDE, HD)) * (inverse * SCALE)
        ob[1, head] = dq.astype(jnp.bfloat16)
        for c in stores(head, (0, 1)):
            c.start()

    def key_side(head):
        for level in (0, 1, 7, 6, 4):
            wait_recv(1, level, head)
        for level in range(FAR):

            @pl.when(me + 2**level < NB)
            def _(level=level):
                stat_copy(level, head).wait_recv()

        k = kv[head, 0, OWN]
        v = kv[head, 1, OWN]
        for slot in range(SLOTS):
            s = dot_nt(k, qg[head, 0, slot]) * (SCALE * LOG2E) - st[head, slot, 0:1, :]
            s = jnp.where(row_id <= col_id, s, NEG) if slot == OWN else s + bias[1, slot]
            p = jnp.exp2(s)
            pb[:, span(slot)] = p.astype(jnp.bfloat16)
            dp = dot_nt(v, qg[head, 1, slot])
            dsb[:, span(slot)] = (p * (dp - st[head, slot, 1:2, :])).astype(jnp.bfloat16)
        ob[3, head] = dot_nn(pb[...], qg[head, 1].reshape(WIDE, HD)).astype(jnp.bfloat16)
        ob[2, head] = (dot_nn(dsb[...], qg[head, 0].reshape(WIDE, HD)) * SCALE).astype(jnp.bfloat16)
        for c in stores(head, (2, 3)):
            c.start()

    @pl.loop(0, H + KEY)
    def _(step):
        for stage, lag in ((own, 0), (relay1, RELAY1), (relay2, RELAY2), (query_side, QUERY), (key_side, KEY)):

            @pl.when((step >= lag) & (step < H + lag))
            def _(stage=stage, lag=lag):
                stage(step - lag)

    for side in range(2):
        m = index[side]
        sent = {0: (m % 4 != 3) | (m >= 4), 1: (m % 4 < 2) | (m >= 4)}
        for level, target, cond in [s for group in (sends_own, sends_near, sends_mid, sends_far) for s in group(side)]:
            if level in (0, 1):
                if level not in sent:
                    continue
                cond = sent.pop(level)

            @pl.when(cond)
            def _(side=side, level=level, target=target):
                pltpu.make_async_remote_copy(
                    src_ref=bufs[side].at[:, :, OWN],
                    dst_ref=bufs[side].at[:, :, level],
                    send_sem=send_sem.at[side, level],
                    recv_sem=recv_sem.at[side, level, 0],
                    device_id=place(real(side, target)),
                    device_id_type=MESH,
                ).wait_send()

    for level in range(FAR):

        @pl.when(me >= 2**level)
        def _(level=level):
            pltpu.make_async_remote_copy(
                src_ref=st.at[:, OWN],
                dst_ref=st.at[:, level],
                send_sem=st_send.at[level],
                recv_sem=st_recv.at[level, 0],
                device_id=place(me - 2**level),
                device_id_type=MESH,
            ).wait_send()

    @pl.loop(0, H)
    def _(head):
        for c in stores(head, range(4)):
            c.wait()


def local(queries, keys, values, grad_out, level_mask):
    any_space = pl.BlockSpec(memory_space=pl.ANY)
    out = jax.ShapeDtypeStruct((BLK, H * HD), jnp.bfloat16)
    return tuple(
        pl.pallas_call(
            kernel,
            name="log_sparse",
            out_shape=(out, out, out, out),
            in_specs=[any_space] * 4 + [pl.BlockSpec(memory_space=pltpu.SMEM)],
            out_specs=(any_space,) * 4,
            scratch_shapes=[
                pltpu.VMEM((H, 2, SLOTS, BLK, HD), jnp.bfloat16),
                pltpu.VMEM((H, 2, SLOTS, BLK, HD), jnp.bfloat16),
                pltpu.VMEM((H, SLOTS, 8, BLK), jnp.float32),
                pltpu.VMEM((BLK, WIDE), jnp.float32),
                pltpu.VMEM((BLK, WIDE), jnp.bfloat16),
                pltpu.VMEM((BLK, WIDE), jnp.bfloat16),
                pltpu.VMEM((4, H, BLK, HD), jnp.bfloat16),
                pltpu.SMEM((2, FAR), jnp.float32),
                pltpu.SemaphoreType.DMA((4, H)),
                pltpu.SemaphoreType.DMA((2, FAR)),
                pltpu.SemaphoreType.DMA((2, FAR, H)),
                pltpu.SemaphoreType.DMA((FAR,)),
                pltpu.SemaphoreType.DMA((FAR, H)),
                pltpu.SemaphoreType.DMA((4, H)),
            ],
            compiler_params=pltpu.CompilerParams(
                collective_id=0, has_side_effects=True, vmem_limit_bytes=48 << 20
            ),
        )(queries, keys, values, grad_out, level_mask)
    )


def solution(mesh):
    rows = P(("ctx", "head"), None)
    return jax.shard_map(
        local,
        mesh=mesh,
        in_specs=(rows, rows, rows, rows, P()),
        out_specs=(rows, rows, rows, rows),
        check_vma=False,
    )
```

time: 654 us -> 236 us (0.36)
  the two profiles are of different devices: /device:TPU:228 before, /device:TPU:2 now
where the time goes in v1:
time: 236 us; the launch traced here: 233 us
  Pallas kernels  224 us (95%)
  local copies, waits for them, and re-layouts  8.16 us (3%)
    pallas_call x1, Pallas kernels, local(): pl.pallas_call(kernel, name='log_sparse', out_shape=(out, out, out, out),...  224 us
    unnamed x13, local copies, waits for them, and re-layouts  8.16 us

profile of v1, /device:TPU:2, one launch (start us, length us, event | category | flops | bytes accessed | tf_op | source)
XLA Modules:
  0.0 232.7 jit_solution(17839546098387321145)
XLA Ops:
  0.6 0.8 copy.9.lm_ref
  1.5 0.0 copy-start
  1.5 1.0 copy-done
  2.5 0.0 copy-start.1
  2.5 1.0 copy-done.1
  3.5 0.0 copy-start.2
  3.5 1.0 copy-done.2
  4.6 0.0 copy-start.3
  4.6 1.0 copy-done.3
  5.6 223.9 %log_sparse.1 = (bf16[128,2048]{1,0:T(8,128)(2,1)S(1)}, bf16[128,2048]{1,0:T(8,128)(2,1)S(1)}, bf16[128,2048]{1,0:T(8,128)(2,1)S(1)}, bf16[128,2048]{1,0:T(8,128)(2,1)S(1)}) custom-call(bf16[128,2048]{1,0:T(8,128)(2,1)S(1)} %copy-done, bf16[128,2048]{1,0:T(8,128)(2,1)S(1)} %copy-done.1, bf16[128,2048]{1,0:T(8,128)(2,1)S(1)} %copy-done.2, ...), custom_call_target="tpu_custom_call" | custom-call | tf_op jit(solution)/shard_map/log_sparse/pallas_call | solution.py:316
  229.5 0.8 copy.14
  230.3 0.8 copy.15
  231.1 0.8 copy.16
  231.9 0.8 copy.17
Async XLA Ops:
  1.5 1.0 copy-start
  2.5 1.0 copy-start.1
  3.5 1.0 copy-start.2
  4.6 1.0 copy-start.3

commit v2 on v1

--- a/solution.py
+++ b/solution.py
@@ -13,16 +13,19 @@
 FAR = 8
 OWN = FAR
 SLOTS = FAR + 1
+SECOND = FAR
 WIDE = SLOTS * BLK
 NEG = -1e30
 SCALE = HD ** (-0.5)
 LOG2E = 1.4426950408889634
 MESH = pl.DeviceIdType.MESH
 
-RELAY1 = 2
-RELAY2 = 4
-QUERY = 6
-KEY = 7
+ROW = 1
+BACK = 2
+NEAR = 3
+FARTHER = 5
+QUERY = 7
+KEY = 8
 
 
 def dot_nt(a, b):
@@ -52,10 +55,12 @@
 
     def copy(side, src, level, head, target):
         buf = bufs[side]
+        slot = level
+        level = 6 if level == SECOND else level
         return pltpu.make_async_remote_copy(
             src_ref=buf.at[head, :, src],
             dst_ref=buf.at[head, :, level],
-            send_sem=send_sem.at[side, level],
+            send_sem=send_sem.at[side, slot],
             recv_sem=recv_sem.at[side, level, head],
             device_id=place(real(side, target)),
             device_id_type=MESH,
@@ -103,53 +108,48 @@
         bias[1, level] = jnp.where((lm_ref[later, level] == 1) & (me + d < NB), 0.0, NEG)
 
     barrier = pltpu.get_barrier_semaphore()
-    count = jnp.where((me % 4 == 0) | (me % 4 == 3), 1, 0)
+    part, line, row = me % 4, (me // 4) % 8, me // 32
+    partners = [(3, part == 0), (-3, part == 3), (28, line == 0), (-28, line == 7)]
+    partners += [(96, row == 4), (-96, row == 7), (96, row == 0), (-96, row == 3)]
     for level in range(FAR):
         d = 2**level
-        count = count + jnp.where(me >= d, 1, 0) + jnp.where(me + d < NB, 1, 0)
-
-        @pl.when(me >= d)
-        def _(d=d):
-            pl.semaphore_signal(barrier, inc=1, device_id=place(me - d), device_id_type=MESH)
-
-        @pl.when(me + d < NB)
+        partners += [(-d, me >= d), (d, me + d < NB)]
+    count = 0
+    for d, cond in partners:
+        count = count + jnp.where(cond, 1, 0)
+
+        @pl.when(cond)
         def _(d=d):
             pl.semaphore_signal(barrier, inc=1, device_id=place(me + d), device_id_type=MESH)
 
-    @pl.when(me % 4 == 0)
-    def _():
-        pl.semaphore_signal(barrier, inc=1, device_id=place(me + 3), device_id_type=MESH)
-
-    @pl.when(me % 4 == 3)
-    def _():
-        pl.semaphore_signal(barrier, inc=1, device_id=place(me - 3), device_id_type=MESH)
-
     pl.semaphore_wait(barrier, count)
 
-    def sends_own(side):
-        m = index[side]
+    def sends_own(m):
+        line, row = (m // 4) % 8, m // 32
         return [
-            (2, m + 4, m + 4 < NB),
-            (5, m + 32, m + 32 < NB),
-            (7, m + 128, m + 128 < NB),
+            (2, m + 4, line < 7),
+            (7, m + 128, row < 4),
+            (5, m + 32, (row != 3) & (row < 7)),
             (0, m + 1, m % 4 != 3),
             (1, m + 2, m % 4 < 2),
         ]
 
-    def sends_near(side):
-        m = index[side]
+    def sends_7(m):
+        row = m // 32
+        return [(5, m - 96, row == 7), (6, m - 64, row == 6)]
+
+    def sends_5(m):
+        line, row = (m // 4) % 8, m // 32
+        return [(2, m - 28, (line == 7) & (row >= 1)), (SECOND, m + 32, (row >= 1) & (row < 7) & (row != 3))]
+
+    def sends_2(m):
         return [
             (3, m + 4, (m >= 4) & (m + 4 < NB)),
             (0, m - 3, (m >= 4) & (m % 4 == 3)),
             (1, m - 2, (m >= 4) & (m % 4 >= 2)),
         ]
 
-    def sends_mid(side):
-        m = index[side]
-        return [(6, m + 32, (m >= 32) & (m + 32 < NB))]
-
-    def sends_far(side):
-        m = index[side]
+    def sends_3(m):
         return [(4, m + 8, (m >= 8) & (m + 8 < NB))]
 
     def own(head):
@@ -157,24 +157,17 @@
             c.wait()
         for i in range(5):
             for side in range(2):
-                level, target, cond = sends_own(side)[i]
+                level, target, cond = sends_own(index[side])[i]
                 send(side, OWN, level, head, target, cond)
 
-    def relay1(head):
-        for side in range(2):
-            wait_recv(side, 2, head)
-            for level, target, cond in sends_near(side):
-                send(side, 2, level, head, target, cond)
-        for side in range(2):
-            wait_recv(side, 5, head)
-            for level, target, cond in sends_mid(side):
-                send(side, 5, level, head, target, cond)
-
-    def relay2(head):
-        for side in range(2):
-            wait_recv(side, 3, head)
-            for level, target, cond in sends_far(side):
-                send(side, 3, level, head, target, cond)
+    def relay(slot, sends):
+        def stage(head):
+            for side in range(2):
+                wait_recv(side, slot, head)
+                for level, target, cond in sends(index[side]):
+                    send(side, slot, level, head, target, cond)
+
+        return stage
 
     def stat_copy(level, head):
         return pltpu.make_async_remote_copy(
@@ -200,7 +193,7 @@
         return pl.ds(slot * BLK, BLK)
 
     def query_side(head):
-        for level in (0, 1, 7, 6, 4):
+        for level in (0, 1, 6, 4):
             wait_recv(0, level, head)
         q = qg[head, 0, OWN]
         g = qg[head, 1, OWN]
@@ -240,7 +233,7 @@
             c.start()
 
     def key_side(head):
-        for level in (0, 1, 7, 6, 4):
+        for level in (0, 1, 6, 4):
             wait_recv(1, level, head)
         for level in range(FAR):
 
@@ -264,7 +257,15 @@
 
     @pl.loop(0, H + KEY)
     def _(step):
-        for stage, lag in ((own, 0), (relay1, RELAY1), (relay2, RELAY2), (query_side, QUERY), (key_side, KEY)):
+        for stage, lag in (
+            (own, 0),
+            (relay(7, sends_7), ROW),
+            (relay(5, sends_5), BACK),
+            (relay(2, sends_2), NEAR),
+            (relay(3, sends_3), FARTHER),
+            (query_side, QUERY),
+            (key_side, KEY),
+        ):
 
             @pl.when((step >= lag) & (step < H + lag))
             def _(stage=stage, lag=lag):
@@ -272,21 +273,28 @@
 
     for side in range(2):
         m = index[side]
-        sent = {0: (m % 4 != 3) | (m >= 4), 1: (m % 4 < 2) | (m >= 4)}
-        for level, target, cond in [s for group in (sends_own, sends_near, sends_mid, sends_far) for s in group(side)]:
-            if level in (0, 1):
-                if level not in sent:
-                    continue
-                cond = sent.pop(level)
+        line, row = (m // 4) % 8, m // 32
+        conds = (
+            (m % 4 != 3) | (m >= 4),
+            (m % 4 < 2) | (m >= 4),
+            (line < 7) | (row >= 1),
+            (m >= 4) & (m + 4 < NB),
+            (m >= 8) & (m + 8 < NB),
+            row != 3,
+            row == 6,
+            row < 4,
+            (row >= 1) & (row < 7) & (row != 3),
+        )
+        for slot, cond in enumerate(conds):
 
             @pl.when(cond)
-            def _(side=side, level=level, target=target):
+            def _(side=side, slot=slot):
                 pltpu.make_async_remote_copy(
                     src_ref=bufs[side].at[:, :, OWN],
-                    dst_ref=bufs[side].at[:, :, level],
-                    send_sem=send_sem.at[side, level],
-                    recv_sem=recv_sem.at[side, level, 0],
-                    device_id=place(real(side, target)),
+                    dst_ref=bufs[side].at[:, :, 0],
+                    send_sem=send_sem.at[side, slot],
+                    recv_sem=recv_sem.at[side, 0, 0],
+                    device_id=place(me),
                     device_id_type=MESH,
                 ).wait_send()
 
@@ -329,7 +337,7 @@
                 pltpu.VMEM((4, H, BLK, HD), jnp.bfloat16),
                 pltpu.SMEM((2, FAR), jnp.float32),
                 pltpu.SemaphoreType.DMA((4, H)),
-                pltpu.SemaphoreType.DMA((2, FAR)),
+                pltpu.SemaphoreType.DMA((2, FAR + 1)),
                 pltpu.SemaphoreType.DMA((2, FAR, H)),
                 pltpu.SemaphoreType.DMA((FAR,)),
                 pltpu.SemaphoreType.DMA((FAR, H)),

time: 236 us -> 172 us (0.73); the launches traced: 233 us -> 172 us
  Pallas kernels: 224 us -> 163 us
    pallas_call x1, Pallas kernels: 224 us -> 163 us  [local(): pl.pallas_call(kernel, name='log_sparse', out_shape=(out, out, out, out),...]
where the time goes in v2:
time: 172 us
  Pallas kernels  163 us (95%)
  local copies, waits for them, and re-layouts  8.16 us (5%)
    pallas_call x1, Pallas kernels, local(): pl.pallas_call(kernel, name='log_sparse', out_shape=(out, out, out, out),...  163 us
    unnamed x13, local copies, waits for them, and re-layouts  8.16 us

profile of v2, /device:TPU:2, one launch (start us, length us, event | category | flops | bytes accessed | tf_op | source)
XLA Modules:
  0.0 171.9 jit_solution(2487440980132113348)
XLA Ops:
  0.6 0.8 copy.9.lm_ref
  1.5 0.0 copy-start
  1.5 1.0 copy-done
  2.5 0.0 copy-start.1
  2.5 1.0 copy-done.1
  3.5 0.0 copy-start.2
  3.5 1.0 copy-done.2
  4.6 0.0 copy-start.3
  4.6 1.0 copy-done.3
  5.6 163.1 %log_sparse.1 = (bf16[128,2048]{1,0:T(8,128)(2,1)S(1)}, bf16[128,2048]{1,0:T(8,128)(2,1)S(1)}, bf16[128,2048]{1,0:T(8,128)(2,1)S(1)}, bf16[128,2048]{1,0:T(8,128)(2,1)S(1)}) custom-call(bf16[128,2048]{1,0:T(8,128)(2,1)S(1)} %copy-done, bf16[128,2048]{1,0:T(8,128)(2,1)S(1)} %copy-done.1, bf16[128,2048]{1,0:T(8,128)(2,1)S(1)} %copy-done.2, ...), custom_call_target="tpu_custom_call" | custom-call | tf_op jit(solution)/shard_map/log_sparse/pallas_call | solution.py:324
  168.8 0.8 copy.14
  169.6 0.8 copy.15
  170.3 0.8 copy.16
  171.1 0.8 copy.17
Async XLA Ops:
  1.5 1.0 copy-start
  2.5 1.0 copy-start.1
  3.5 1.0 copy-start.2
  4.6 1.0 copy-start.3

commit v3 on v2

--- a/solution.py
+++ b/solution.py
@@ -23,8 +23,8 @@
 ROW = 1
 BACK = 2
 NEAR = 3
-FARTHER = 5
-QUERY = 7
+FARTHER = 4
+QUERY = 5
 KEY = 8
 
 
@@ -43,7 +43,7 @@
 def kernel(
     q_hbm, k_hbm, v_hbm, g_hbm, lm_ref,
     o_hbm, dq_hbm, dk_hbm, dv_hbm,
-    kv, qg, st, p_s, pb, dsb, ob, bias,
+    kv, qg, st, p_s, pb, dsb, pk, dsk, ob, bias,
     load_sem, send_sem, recv_sem, st_send, st_recv, out_sem,
 ):
     me = lax.axis_index("ctx") * 2 + lax.axis_index("head")
@@ -90,17 +90,6 @@
         for c in loads(head):
             c.start()
 
-    for side in range(2):
-        for level in range(FAR):
-
-            @pl.when(index[side] < 2**level)
-            def _(side=side, level=level):
-                @pl.loop(0, H)
-                def _(head):
-                    bufs[side][head, :, level] = jnp.zeros((2, BLK, HD), jnp.bfloat16)
-                    if side == 1:
-                        st[head, level] = jnp.zeros((8, BLK), jnp.float32)
-
     for level in range(FAR):
         d = 2**level
         bias[0, level] = jnp.where((lm_ref[me, level] == 1) & (me >= d), 0.0, NEG)
@@ -155,6 +144,17 @@
     def own(head):
         for c in loads(head):
             c.wait()
+        send_own(head)
+        for side in range(2):
+            for level in range(FAR):
+
+                @pl.when(index[side] < 2**level)
+                def _(side=side, level=level):
+                    bufs[side][head, :, level] = jnp.zeros((2, BLK, HD), jnp.bfloat16)
+                    if side == 1:
+                        st[head, level] = jnp.zeros((8, BLK), jnp.float32)
+
+    def send_own(head):
         for i in range(5):
             for side in range(2):
                 level, target, cond = sends_own(index[side])[i]
@@ -192,9 +192,20 @@
     def span(slot):
         return pl.ds(slot * BLK, BLK)
 
-    def query_side(head):
+    def query_waits(head):
         for level in (0, 1, 6, 4):
             wait_recv(0, level, head)
+
+    def key_waits(head):
+        for level in (0, 1, 6, 4):
+            wait_recv(1, level, head)
+        for level in range(FAR):
+
+            @pl.when(me + 2**level < NB)
+            def _(level=level):
+                stat_copy(level, head).wait_recv()
+
+    def query_parts(head):
         q = qg[head, 0, OWN]
         g = qg[head, 1, OWN]
         top = None
@@ -203,13 +214,16 @@
             s = jnp.where(row_id >= col_id, s, NEG) if slot == OWN else s + bias[0, slot]
             p_s[:, span(slot)] = s
             top = s if top is None else jnp.maximum(top, s)
+            yield
         top = jnp.max(top, axis=1, keepdims=True)
+        yield
         total = None
         for slot in range(SLOTS):
             p = jnp.exp2(p_s[:, span(slot)] - top)
             p_s[:, span(slot)] = p
             pb[:, span(slot)] = p.astype(jnp.bfloat16)
             total = p if total is None else total + p
+            yield
         total = jnp.sum(total, axis=1, keepdims=True)
         inverse = 1.0 / total
         o = dot_nn(pb[...], kv[head, 1].reshape(WIDE, HD)) * inverse
@@ -217,43 +231,68 @@
         ob[0, head] = o
         delta = jnp.sum(g.astype(jnp.float32) * o.astype(jnp.float32), axis=1, keepdims=True)
         lse = top + jnp.log2(total)
+        yield
+        for slot in range(SLOTS):
+            dp = dot_nt(g, kv[head, 1, slot])
+            dsb[:, span(slot)] = (p_s[:, span(slot)] * (dp - delta)).astype(jnp.bfloat16)
+            yield
+        dq = dot_nn(dsb[...], kv[head, 0].reshape(WIDE, HD)) * (inverse * SCALE)
+        ob[1, head] = dq.astype(jnp.bfloat16)
         st[head, OWN] = jnp.where(col_id == 0, lse, delta).T[:8]
+
+    def query_done(head):
         for level in range(FAR):
 
             @pl.when(me >= 2**level)
             def _(level=level):
                 stat_copy(level, head).start()
 
-        for slot in range(SLOTS):
-            dp = dot_nt(g, kv[head, 1, slot])
-            dsb[:, span(slot)] = (p_s[:, span(slot)] * (dp - delta)).astype(jnp.bfloat16)
-        dq = dot_nn(dsb[...], kv[head, 0].reshape(WIDE, HD)) * (inverse * SCALE)
-        ob[1, head] = dq.astype(jnp.bfloat16)
         for c in stores(head, (0, 1)):
             c.start()
 
-    def key_side(head):
-        for level in (0, 1, 6, 4):
-            wait_recv(1, level, head)
-        for level in range(FAR):
-
-            @pl.when(me + 2**level < NB)
-            def _(level=level):
-                stat_copy(level, head).wait_recv()
-
+    def key_parts(head):
         k = kv[head, 0, OWN]
         v = kv[head, 1, OWN]
         for slot in range(SLOTS):
             s = dot_nt(k, qg[head, 0, slot]) * (SCALE * LOG2E) - st[head, slot, 0:1, :]
             s = jnp.where(row_id <= col_id, s, NEG) if slot == OWN else s + bias[1, slot]
             p = jnp.exp2(s)
-            pb[:, span(slot)] = p.astype(jnp.bfloat16)
+            pk[:, span(slot)] = p.astype(jnp.bfloat16)
+            yield
             dp = dot_nt(v, qg[head, 1, slot])
-            dsb[:, span(slot)] = (p * (dp - st[head, slot, 1:2, :])).astype(jnp.bfloat16)
-        ob[3, head] = dot_nn(pb[...], qg[head, 1].reshape(WIDE, HD)).astype(jnp.bfloat16)
-        ob[2, head] = (dot_nn(dsb[...], qg[head, 0].reshape(WIDE, HD)) * SCALE).astype(jnp.bfloat16)
+            dsk[:, span(slot)] = (p * (dp - st[head, slot, 1:2, :])).astype(jnp.bfloat16)
+            yield
+        ob[3, head] = dot_nn(pk[...], qg[head, 1].reshape(WIDE, HD)).astype(jnp.bfloat16)
+        yield
+        ob[2, head] = (dot_nn(dsk[...], qg[head, 0].reshape(WIDE, HD)) * SCALE).astype(jnp.bfloat16)
+
+    def key_done(head):
         for c in stores(head, (2, 3)):
             c.start()
+
+    def together(*parts):
+        parts = list(parts)
+        while parts:
+            for part in tuple(parts):
+                if next(part, True):
+                    parts.remove(part)
+
+    def query_side(head):
+        query_waits(head)
+        together(query_parts(head))
+        query_done(head)
+
+    def key_side(head):
+        key_waits(head)
+        together(key_parts(head))
+        key_done(head)
+
+    def both_sides(head, key_head):
+        query_waits(head)
+        key_waits(key_head)
+        together(query_parts(head), key_parts(key_head))
+        query_done(head)
+        key_done(key_head)
 
     @pl.loop(0, H + KEY)
     def _(step):
@@ -263,13 +302,23 @@
             (relay(5, sends_5), BACK),
             (relay(2, sends_2), NEAR),
             (relay(3, sends_3), FARTHER),
-            (query_side, QUERY),
-            (key_side, KEY),
         ):
 
             @pl.when((step >= lag) & (step < H + lag))
             def _(stage=stage, lag=lag):
                 stage(step - lag)
+
+        @pl.when((step >= KEY) & (step < H + QUERY))
+        def _():
+            both_sides(step - QUERY, step - KEY)
+
+        @pl.when((step >= QUERY) & (step < KEY))
+        def _():
+            query_side(step - QUERY)
+
+        @pl.when(step >= H + QUERY)
+        def _():
+            key_side(step - KEY)
 
     for side in range(2):
         m = index[side]
@@ -318,20 +367,22 @@
 
 
 def local(queries, keys, values, grad_out, level_mask):
-    any_space = pl.BlockSpec(memory_space=pl.ANY)
+    hbm = pl.BlockSpec(memory_space=pltpu.HBM)
     out = jax.ShapeDtypeStruct((BLK, H * HD), jnp.bfloat16)
     return tuple(
         pl.pallas_call(
             kernel,
             name="log_sparse",
             out_shape=(out, out, out, out),
-            in_specs=[any_space] * 4 + [pl.BlockSpec(memory_space=pltpu.SMEM)],
-            out_specs=(any_space,) * 4,
+            in_specs=[hbm] * 4 + [pl.BlockSpec(memory_space=pltpu.SMEM)],
+            out_specs=(hbm,) * 4,
             scratch_shapes=[
                 pltpu.VMEM((H, 2, SLOTS, BLK, HD), jnp.bfloat16),
                 pltpu.VMEM((H, 2, SLOTS, BLK, HD), jnp.bfloat16),
                 pltpu.VMEM((H, SLOTS, 8, BLK), jnp.float32),
                 pltpu.VMEM((BLK, WIDE), jnp.float32),
+                pltpu.VMEM((BLK, WIDE), jnp.bfloat16),
+                pltpu.VMEM((BLK, WIDE), jnp.bfloat16),
                 pltpu.VMEM((BLK, WIDE), jnp.bfloat16),
                 pltpu.VMEM((BLK, WIDE), jnp.bfloat16),
                 pltpu.VMEM((4, H, BLK, HD), jnp.bfloat16),
@@ -344,7 +395,7 @@
                 pltpu.SemaphoreType.DMA((4, H)),
             ],
             compiler_params=pltpu.CompilerParams(
-                collective_id=0, has_side_effects=True, vmem_limit_bytes=48 << 20
+                collective_id=0, has_side_effects=True, vmem_limit_bytes=63 << 20
             ),
         )(queries, keys, values, grad_out, level_mask)
     )

time: 172 us -> 163 us (0.948)
  Pallas kernels: 163 us -> 155 us
    pallas_call x1, Pallas kernels: 163 us -> 155 us  [local(): pl.pallas_call(kernel, name='log_sparse', out_shape=(out, out, out, out),...]
    unnamed x13 -> x11, local copies, waits for them, and re-layouts: 8.16 us -> 6.68 us
where the time goes in v3:
time: 163 us; the launch traced here: 162 us
  Pallas kernels  155 us (95%)
  local copies, waits for them, and re-layouts  6.68 us (4%)
    pallas_call x1, Pallas kernels, local(): pl.pallas_call(kernel, name='log_sparse', out_shape=(out, out, out, out),...  155 us
    unnamed x11, local copies, waits for them, and re-layouts  6.68 us

profile of v3, /device:TPU:2, one launch (start us, length us, event | category | flops | bytes accessed | tf_op | source)
XLA Modules:
  0.0 162.3 jit_solution(6840341676863599316)
XLA Ops:
  0.6 1.5 copy.9.lm_ref
  2.1 155.0 %log_sparse.1 = (bf16[128,2048]{1,0:T(8,128)(2,1)}, bf16[128,2048]{1,0:T(8,128)(2,1)}, bf16[128,2048]{1,0:T(8,128)(2,1)}, bf16[128,2048]{1,0:T(8,128)(2,1)}) custom-call(bf16[128,2048]{1,0:T(8,128)(2,1)} %q_hbm.1, bf16[128,2048]{1,0:T(8,128)(2,1)} %k_hbm.1, bf16[128,2048]{1,0:T(8,128)(2,1)} %v_hbm.1, bf16[128,2048]{1,0:T(8,128)(2,1)} %g_hbm.1, ...), custom_call_target="tpu_custom_call" | custom-call | tf_op jit(solution)/shard_map/log_sparse/pallas_call | solution.py:373
  157.1 0.0 copy-start.2
  157.1 1.9 %copy.14 = bf16[128,2048]{1,0:T(8,128)(2,1)} copy(bf16[128,2048]{1,0:T(8,128)(2,1)} %get-tuple-element.8) | data formatting | bytes 1048576
  159.1 0.0 copy-done.2
  159.1 0.0 copy-start.1
  159.1 0.8 copy.15
  159.9 0.4 copy-done.1
  160.3 0.0 copy-start
  160.3 0.8 copy.16
  161.1 0.4 copy-done
  161.5 0.8 copy.17
Async XLA Ops:
  157.1 2.0 %copy-start.2 = (bf16[128,2048]{1,0:T(8,128)(2,1)S(1)}, bf16[128,2048]{1,0:T(8,128)(2,1)}, u32[]{:S(2)}) copy-start(bf16[128,2048]{1,0:T(8,128)(2,1)} %get-tuple-element.9) | copy-start | bytes 1572868
  159.1 1.2 copy-start.1
  160.3 1.2 copy-start

commit v4 on v3

--- a/solution.py
+++ b/solution.py
@@ -92,9 +92,9 @@
 
     for level in range(FAR):
         d = 2**level
-        bias[0, level] = jnp.where((lm_ref[me, level] == 1) & (me >= d), 0.0, NEG)
+        bias[0, level] = jnp.where((lm_ref[level, me] == 1) & (me >= d), 0.0, NEG)
         later = jnp.minimum(me + d, NB - 1)
-        bias[1, level] = jnp.where((lm_ref[later, level] == 1) & (me + d < NB), 0.0, NEG)
+        bias[1, level] = jnp.where((lm_ref[level, later] == 1) & (me + d < NB), 0.0, NEG)
 
     barrier = pltpu.get_barrier_semaphore()
     part, line, row = me % 4, (me // 4) % 8, me // 32
@@ -397,7 +397,7 @@
             compiler_params=pltpu.CompilerParams(
                 collective_id=0, has_side_effects=True, vmem_limit_bytes=63 << 20
             ),
-        )(queries, keys, values, grad_out, level_mask)
+        )(queries, keys, values, grad_out, level_mask.T)
     )
 
 

time: 163 us -> 162 us (level)
    unnamed x11 -> x10, local copies, waits for them, and re-layouts: 6.68 us -> 5.19 us
where the time goes in v4:
time: 162 us; the launch traced here: 161 us
  Pallas kernels  155 us (96%)
  local copies, waits for them, and re-layouts  5.19 us (3%)
    pallas_call x1, Pallas kernels, local(): pl.pallas_call(kernel, name='log_sparse', out_shape=(out, out, out, out),...  155 us
    unnamed x10, local copies, waits for them, and re-layouts  5.19 us

profile of v4, /device:TPU:2, one launch (start us, length us, event | category | flops | bytes accessed | tf_op | source)
XLA Modules:
  0.0 161.3 jit_solution(14684327121909854533)
XLA Ops:
  0.6 155.5 %log_sparse.1 = (bf16[128,2048]{1,0:T(8,128)(2,1)}, bf16[128,2048]{1,0:T(8,128)(2,1)}, bf16[128,2048]{1,0:T(8,128)(2,1)}, bf16[128,2048]{1,0:T(8,128)(2,1)}) custom-call(bf16[128,2048]{1,0:T(8,128)(2,1)} %q_hbm.1, bf16[128,2048]{1,0:T(8,128)(2,1)} %k_hbm.1, bf16[128,2048]{1,0:T(8,128)(2,1)} %v_hbm.1, bf16[128,2048]{1,0:T(8,128)(2,1)} %g_hbm.1, s32[9,256]{1,0:T(8,128)} %bitcast.1), custom_call_target="tpu_custom_call" | custom-call | tf_op jit(solution)/shard_map/log_sparse/pallas_call | solution.py:373
  156.1 0.0 copy-start.2
  156.1 1.9 %copy.13 = bf16[128,2048]{1,0:T(8,128)(2,1)} copy(bf16[128,2048]{1,0:T(8,128)(2,1)} %get-tuple-element.8) | data formatting | bytes 1048576
  158.1 0.0 copy-done.2
  158.1 0.0 copy-start.1
  158.1 0.8 copy.14
  158.9 0.4 copy-done.1
  159.3 0.0 copy-start
  159.3 0.8 copy.15
  160.1 0.4 copy-done
  160.5 0.8 copy.16
Async XLA Ops:
  156.1 2.0 %copy-start.2 = (bf16[128,2048]{1,0:T(8,128)(2,1)S(1)}, bf16[128,2048]{1,0:T(8,128)(2,1)}, u32[]{:S(2)}) copy-start(bf16[128,2048]{1,0:T(8,128)(2,1)} %get-tuple-element.9) | copy-start | bytes 1572868
  158.1 1.2 copy-start.1
  159.3 1.2 copy-start

commit v5 on v4

--- a/solution.py
+++ b/solution.py
@@ -119,8 +119,6 @@
             (2, m + 4, line < 7),
             (7, m + 128, row < 4),
             (5, m + 32, (row != 3) & (row < 7)),
-            (0, m + 1, m % 4 != 3),
-            (1, m + 2, m % 4 < 2),
         ]
 
     def sends_7(m):
@@ -155,7 +153,7 @@
                         st[head, level] = jnp.zeros((8, BLK), jnp.float32)
 
     def send_own(head):
-        for i in range(5):
+        for i in range(3):
             for side in range(2):
                 level, target, cond = sends_own(index[side])[i]
                 send(side, OWN, level, head, target, cond)
@@ -166,6 +164,10 @@
                 wait_recv(side, slot, head)
                 for level, target, cond in sends(index[side]):
                     send(side, slot, level, head, target, cond)
+                if slot == 2:
+                    m = index[side]
+                    send(side, OWN, 0, head, m + 1, m % 4 != 3)
+                    send(side, OWN, 1, head, m + 2, m % 4 < 2)
 
         return stage
 

time: 162 us -> 158 us (0.975)
  Pallas kernels: 155 us -> 150 us
    pallas_call x1, Pallas kernels: 155 us -> 150 us  [local(): pl.pallas_call(kernel, name='log_sparse', out_shape=(out, out, out, out),...]
where the time goes in v5:
time: 158 us; the launch traced here: 156 us
  Pallas kernels  150 us (95%)
  local copies, waits for them, and re-layouts  5.19 us (3%)
    pallas_call x1, Pallas kernels, local(): pl.pallas_call(kernel, name='log_sparse', out_shape=(out, out, out, out),...  150 us
    unnamed x10, local copies, waits for them, and re-layouts  5.19 us

profile of v5, /device:TPU:2, one launch (start us, length us, event | category | flops | bytes accessed | tf_op | source)
XLA Modules:
  0.0 155.7 jit_solution(16416245009445508754)
XLA Ops:
  0.6 149.9 %log_sparse.1 = (bf16[128,2048]{1,0:T(8,128)(2,1)}, bf16[128,2048]{1,0:T(8,128)(2,1)}, bf16[128,2048]{1,0:T(8,128)(2,1)}, bf16[128,2048]{1,0:T(8,128)(2,1)}) custom-call(bf16[128,2048]{1,0:T(8,128)(2,1)} %q_hbm.1, bf16[128,2048]{1,0:T(8,128)(2,1)} %k_hbm.1, bf16[128,2048]{1,0:T(8,128)(2,1)} %v_hbm.1, bf16[128,2048]{1,0:T(8,128)(2,1)} %g_hbm.1, s32[9,256]{1,0:T(8,128)} %bitcast.1), custom_call_target="tpu_custom_call" | custom-call | tf_op jit(solution)/shard_map/log_sparse/pallas_call | solution.py:375
  150.5 0.0 copy-start.2
  150.5 1.9 %copy.13 = bf16[128,2048]{1,0:T(8,128)(2,1)} copy(bf16[128,2048]{1,0:T(8,128)(2,1)} %get-tuple-element.8) | data formatting | bytes 1048576
  152.5 0.0 copy-done.2
  152.5 0.0 copy-start.1
  152.5 0.8 copy.14
  153.3 0.4 copy-done.1
  153.7 0.0 copy-start
  153.7 0.8 copy.15
  154.5 0.4 copy-done
  154.9 0.8 copy.16
Async XLA Ops:
  150.5 2.0 %copy-start.2 = (bf16[128,2048]{1,0:T(8,128)(2,1)S(1)}, bf16[128,2048]{1,0:T(8,128)(2,1)}, u32[]{:S(2)}) copy-start(bf16[128,2048]{1,0:T(8,128)(2,1)} %get-tuple-element.9) | copy-start | bytes 1572868
  152.5 1.2 copy-start.1
  153.7 1.2 copy-start
